TPU v7x, 32 devices: a whole 2x2x4 slice. The times are simulated.
32 devices in a mesh: row: 8 (over z, core), col: 4 (over y, x).
Axes of the slice: x: 2, y: 2, z: 4, core: 2. Of those that a mesh axis runs over, the one named last changes fastest.
Arguments:
- amplitudes: bfloat16 [256, 4, 16384], P('col', None, 'row'), may hold values from -6 to 6
- integrals: bfloat16 [4, 16384, 16384], P(None, 'row', 'col'), may hold values from -0.046875 to 0.046875
- block_sizes: int32 [4], replicated, may hold values from 8192 to 16384, as said below
Outputs:
- ladder: float32 [256, 4, 16384], P('row', None, 'col')
Inputs may be any that keep to these rules, and one draw needn't show every extreme that they name: Each irrep block uses its first block_sizes[h] pairs; in every draw some block uses all 16384.
All inputs are finite; a program needn't handle non-finite values.
Results may differ from a plain program's by a relative error of at most 0.0003.
Values may be sent and summed in bfloat16 or wider, within the bound.
A program may use at most 128 MiB of HBM per device.

v0:
```python
import functools

import jax
import jax.numpy as jnp
from jax import lax
from jax.experimental import pallas as pl
from jax.experimental.pallas import tpu as pltpu
from jax.sharding import PartitionSpec as P

CORES = 2
SLOTS = 4
TILE = 256
LAG = 2
TOP = 32766.0
TINY = 1e-30


def kernel(chips, cols, steps, chunk, sizes, amp, integ, out, gathered, masked, panel, part, peer, stage, inbox,
           scale_out, scale_in, own_sem, gather_send, gather_recv, panel_sem, peer_send, peer_recv,
           stage_send, inbox_recv, scale_send, scale_recv):
    row, col = lax.axis_index("row"), lax.axis_index("col")
    z, core = row // CORES, row % CORES
    blocks, _, pairs, span = amp.shape
    per_block = steps // blocks
    early = min(per_block, SLOTS)
    width = chunk * per_block
    mate = z * CORES + 1 - core

    def send(src, dst, send_sem, recv_sem, to_row, to_col):
        return pltpu.make_async_remote_copy(
            src_ref=src, dst_ref=dst, send_sem=send_sem, recv_sem=recv_sem,
            device_id={"row": to_row, "col": to_col}, device_id_type=pl.DeviceIdType.MESH)

    def panel_copy(t):
        lanes = pl.ds(pl.multiple_of((t % per_block) * chunk, chunk), chunk)
        slot = t % SLOTS
        return pltpu.make_async_copy(integ.at[t // per_block, :, lanes], panel.at[slot], panel_sem.at[slot])

    def gather_copy(h, q, k):
        return send(amp.at[h, q], gathered.at[h, q, col], gather_send.at[h, q, k], gather_recv.at[h, q, col],
                    row, (col + k) % cols)

    def gather_wait(h, q, k):
        source = (col + k) % cols
        send(amp.at[h, q], gathered.at[h, q, source], gather_send.at[h, q, k], gather_recv.at[h, q, source],
             row, source).wait_recv()

    def own_copy(h, q):
        return pltpu.make_async_copy(amp.at[h, q], gathered.at[h, q, col], own_sem.at[h, q])

    def peer_copy(t):
        return send(part.at[t, 1 - core], peer.at[t], peer_send.at[t], peer_recv.at[t], mate, col)

    def data_copy(t, d, way, to_row):
        slot = d + 1 - way
        return send(stage.at[t, d], inbox.at[t, slot], stage_send.at[t, d], inbox_recv.at[t, slot], to_row, col)

    def scale_copy(t, way, to_row):
        return send(scale_out.at[way, t], scale_in.at[way, t], scale_send.at[way, t], scale_recv.at[way, t], to_row, col)

    def loop(low, high, body):
        lax.fori_loop(low, high, lambda i, c: (body(i), c)[1], 0)

    for t in range(min(SLOTS, steps)):
        panel_copy(t).start()
    loop(0, blocks, lambda h: loop(0, CORES, lambda q: own_copy(h, q).start()))

    barrier = pltpu.get_barrier_semaphore()

    def greet(to_row, to_col):
        pl.semaphore_signal(barrier, inc=1, device_id={"row": to_row, "col": to_col},
                            device_id_type=pl.DeviceIdType.MESH)

    loop(1, cols, lambda k: greet(row, (col + k) % cols))
    greet(mate, col)

    @pl.when(z > 0)
    def _():
        greet(row - CORES, col)

    @pl.when(z < chips - 1)
    def _():
        greet(row + CORES, col)

    pl.semaphore_wait(barrier, cols + jnp.where(z > 0, 1, 0) + jnp.where(z < chips - 1, 1, 0))

    loop(0, blocks, lambda h: loop(0, CORES, lambda q: loop(1, cols, lambda k: gather_copy(h, q, k).start())))

    def prepare(h, q):
        own_copy(h, q).wait()
        loop(1, cols, lambda k: gather_wait(h, q, k))
        index = row * span + lax.broadcasted_iota(jnp.int32, (pairs, span), 1)
        live = index < sizes[h]

        def fill(c):
            values = jnp.where(live, gathered[h, q, c].astype(jnp.float32), 0.0)
            masked[q, pl.ds(pl.multiple_of(c * pairs, pairs), pairs), :] = values.astype(masked.dtype)

        loop(0, cols, fill)

    def next_panel(t):
        @pl.when(t + SLOTS < steps)
        def _():
            panel_copy(t + SLOTS).start()

    def half(t, q):
        @pl.when(t == 0)
        def _():
            prepare(0, q)

        @pl.when(q == 0)
        def _():
            panel_copy(t).wait()

        slot = t % SLOTS

        def tile(n):
            lanes = pl.ds(pl.multiple_of(n * TILE, TILE), TILE)
            value = jnp.dot(masked[q], panel[slot, :, lanes], preferred_element_type=jnp.float32)
            part[t, q, :, :, lanes] = value.reshape(chips, pairs, TILE)

        loop(0, chunk // TILE, tile)

        @pl.when(core != q)
        def _():
            peer_copy(t).start()

        @pl.when(q == 1)
        def _():
            next_panel(t)

    def full(t):
        @pl.when(t % per_block == 0)
        def _():
            loop(0, CORES, lambda q: prepare(t // per_block, q))

        panel_copy(t).wait()
        slot = t % SLOTS

        def tile(n):
            lanes = pl.ds(pl.multiple_of(n * TILE, TILE), TILE)
            left = masked[...].reshape(CORES * chips * pairs, span)
            value = jnp.dot(left, panel[slot, :, lanes], preferred_element_type=jnp.float32)
            part[t, :, :, :, lanes] = value.reshape(CORES, chips, pairs, TILE)

        loop(0, chunk // TILE, tile)
        peer_copy(t).start()
        next_panel(t)

    def combine(t):
        peer_copy(t).wait_recv()

        def add(d):
            part[t, core, d] = part[t, core, d] + peer[t, d]

        loop(0, chips, add)

    def relay(t, way):
        up = way == 0
        has_source = z > 0 if up else z < chips - 1
        has_target = z < chips - 1 if up else z > 0
        to_row = row + CORES if up else row - CORES
        first, last = (z + 1, chips) if up else (0, z)

        @pl.when(has_source)
        def _():
            scale_copy(t, way, row).wait_recv()
            factor = scale_in[way, t]

            def take(d):
                data_copy(t, d, way, row).wait_recv()
                part[t, core, d] = part[t, core, d] + inbox[t, d + 1 - way].astype(jnp.int32).astype(jnp.float32) * factor

            loop(*((z, chips) if up else (0, z + 1)), take)

        @pl.when(has_target)
        def _():
            largest = lax.fori_loop(
                first, last,
                lambda d, m: jnp.maximum(m, jnp.max(jnp.abs(part[t, core, d]), axis=0, keepdims=True)),
                jnp.full((1, chunk), TINY, jnp.float32))
            scale_out[way, t] = largest * (1.0 / TOP)
            scale_copy(t, way, to_row).start()
            inverse = TOP / largest

            def put(d):
                stage[t, d] = jnp.round(part[t, core, d] * inverse).astype(jnp.int32).astype(jnp.int16)
                data_copy(t, d, way, to_row).start()

            loop(0, last - first, (lambda j: put(last - 1 - j)) if up else put)

    def finish(t):
        h = t // per_block
        low = (t % per_block) * chunk
        index = col * width + low + lax.broadcasted_iota(jnp.int32, (pairs, chunk), 1)
        out[h, :, pl.ds(pl.multiple_of(low, chunk), chunk)] = jnp.where(index < sizes[h], part[t, core, z], 0.0)

    def when(condition, body, *args):
        @pl.when(condition)
        def _():
            body(*args)

    def at(j, body):
        ahead = jnp.logical_and(core == 0, j < early)
        t = jnp.where(ahead, j, jnp.where(jnp.logical_and(core == 0, j < 2 * early), -1, j - early))
        when(jnp.logical_and(t >= 0, t < steps), body, t)

    up_lag = 1 + LAG * z
    down_lag = 1 + LAG * (chips - 1 - z)
    end_lag = 1 + LAG * chips

    def step(i):
        when(jnp.logical_and(i < 2 * early, i != early), lambda: half(i % early, i // early))
        when(jnp.logical_and(i >= 2 * early, i < steps + early), lambda: full(i - early))
        at(i - 1, combine)
        at(i - up_lag, lambda t: relay(t, 0))
        at(i - down_lag, lambda t: relay(t, 1))
        at(i - end_lag, finish)
        when(i == early, lambda: half(0, 1))

    loop(0, steps + early + end_lag, step)

    loop(0, blocks, lambda h: loop(0, CORES, lambda q: loop(1, cols, lambda k: gather_copy(h, q, k).wait_send())))

    def drain(t):
        peer_copy(t).wait_send()

        @pl.when(z < chips - 1)
        def _():
            scale_copy(t, 0, row).wait_send()
            loop(z + 1, chips, lambda d: data_copy(t, d, 0, row).wait_send())

        @pl.when(z > 0)
        def _():
            scale_copy(t, 1, row).wait_send()
            loop(0, z, lambda d: data_copy(t, d, 1, row).wait_send())

    loop(0, steps, drain)


def body(chips, cols, amplitudes, integrals, block_sizes):
    share, blocks, span = amplitudes.shape
    width = integrals.shape[2]
    chunk = min(1024, width)
    steps = blocks * (width // chunk)
    total = share * cols
    pairs = total // (chips * CORES)
    assert share == CORES * pairs and chips == cols
    dma = pltpu.SemaphoreType.DMA
    result = pl.pallas_call(
        functools.partial(kernel, chips, cols, steps, chunk),
        out_shape=jax.ShapeDtypeStruct((blocks, pairs, width), jnp.float32),
        in_specs=[
            pl.BlockSpec(memory_space=pltpu.SMEM),
            pl.BlockSpec(memory_space=pl.ANY),
            pl.BlockSpec(memory_space=pl.ANY),
        ],
        out_specs=pl.BlockSpec(memory_space=pltpu.VMEM),
        scratch_shapes=[
            pltpu.VMEM((blocks, CORES, cols, pairs, span), amplitudes.dtype),
            pltpu.VMEM((CORES, chips * pairs, span), amplitudes.dtype),
            pltpu.VMEM((SLOTS, span, chunk), integrals.dtype),
            pltpu.VMEM((steps, CORES, chips, pairs, chunk), jnp.float32),
            pltpu.VMEM((steps, chips, pairs, chunk), jnp.float32),
            pltpu.VMEM((steps, chips, pairs, chunk), jnp.int16),
            pltpu.VMEM((steps, chips + 1, pairs, chunk), jnp.int16),
            pltpu.VMEM((2, steps, 1, chunk), jnp.float32),
            pltpu.VMEM((2, steps, 1, chunk), jnp.float32),
            dma((blocks, CORES)),
            dma((blocks, CORES, cols)),
            dma((blocks, CORES, cols)),
            dma((SLOTS,)),
            dma((steps,)),
            dma((steps,)),
            dma((steps, chips)),
            dma((steps, chips + 1)),
            dma((2, steps)),
            dma((2, steps)),
        ],
        compiler_params=pltpu.CompilerParams(
            collective_id=0, has_side_effects=True, vmem_limit_bytes=63 * 2**20
        ),
        name="ladder",
    )(block_sizes, amplitudes.reshape(CORES, pairs, blocks, span).transpose(2, 0, 1, 3), integrals)
    return result.transpose(1, 0, 2)


def solution(mesh):
    placed = (P("col", None, "row"), P(None, "row", "col"), P())
    return jax.shard_map(
        functools.partial(body, mesh.shape["row"] // CORES, mesh.shape["col"]),
        mesh=mesh, in_specs=placed, out_specs=P("row", None, "col"), check_vma=False,
    )
```

profile of v0, /device:TPU:0, one launch (start us, length us, event | category | flops | bytes accessed | tf_op | source)
XLA Modules:
  0.0 108.5 jit_solution(15906884050247944210)
XLA Ops:
  0.0 2.8 %copy.4 = bf16[64,4,2048]{2,0,1:T(8,128)(2,1)} copy(bf16[64,4,2048]{2,1,0:T(4,128)(2,1)} %param.3) | data formatting | bytes 2097152 | tf_op args[0]
  2.8 101.4 %ladder.1 = f32[4,32,4096]{2,1,0:T(8,128)} custom-call(s32[4]{0:T(128)} %sizes.1, bf16[4,2,32,2048]{3,2,1,0:T(8,128)(2,1)} %bitcast.5, bf16[4,2048,4096]{2,1,0:T(8,128)(2,1)} %integ.1), custom_call_target="tpu_custom_call" | custom-call | tf_op jit(solution)/shard_map/ladder/pallas_call | solution.py:250
  104.2 4.3 %copy.5 = f32[32,4,4096]{2,1,0:T(4,128)} copy(f32[32,4,4096]{2,0,1:T(8,128)} %bitcast.4) | data formatting | bytes 4194304 | tf_op jit(solution)/shard_map/transpose | solution.py:285
where the time goes:
time: 109 us; the launch traced here: 108 us
  Pallas kernels  101 us (93%)
  local copies, waits for them, and re-layouts  7.03 us (6%)
    pallas_call x1, Pallas kernels, body(): pl.pallas_call(functools.partial(kernel, chips, cols, steps, chunk), out_...  101 us
    transpose x1, local copies, waits for them, and re-layouts, body(): return result.transpose(1, 0, 2)  4.26 us
    unnamed x1, local copies, waits for them, and re-layouts  2.77 us

commit v1 on v0

v1 whole, which is shorter than its diff:
```python
import functools
import math

import jax
import jax.numpy as jnp
from jax import lax
from jax.experimental import pallas as pl
from jax.experimental.pallas import tpu as pltpu
from jax.sharding import PartitionSpec as P

CORES = 2
CHUNK = 512
SLOTS = 8
LANES = 128
LAG = 3
RING = 2 * LAG + 6
TOP = 32766.0
TINY = 1e-30


def kernel(chips, cols, steps, chunk, sizes, amp, integ, out, raw, gathered, panel, part, peer, stage, inbox,
           scale_out, scale_in, raw_sem, gather_send, gather_recv, panel_sem, peer_send, peer_recv,
           stage_send, inbox_recv, scale_send, scale_recv):
    row, col = lax.axis_index("row"), lax.axis_index("col")
    z, core = row // CORES, row % CORES
    share, blocks, span = amp.shape
    pairs = share // CORES
    per_block = steps // blocks
    slots, peers, ring = panel.shape[0], peer.shape[0], stage.shape[0]
    early = min(per_block, slots)
    width = chunk * per_block
    mate = z * CORES + 1 - core
    side = math.isqrt(cols)
    shifts = sorted(((a, b) for a in range(side) for b in range(side) if a or b), key=lambda s: (sum(map(bool, s)), s))

    def partner(shift, sign):
        a, b = (sign * s + side for s in shift)
        return (col // side + a) % side * side + (col % side + b) % side

    def send(src, dst, send_sem, recv_sem, to_row, to_col):
        return pltpu.make_async_remote_copy(
            src_ref=src, dst_ref=dst, send_sem=send_sem, recv_sem=recv_sem,
            device_id={"row": to_row, "col": to_col}, device_id_type=pl.DeviceIdType.MESH)

    def panel_copy(t):
        lanes = pl.ds(pl.multiple_of((t % per_block) * chunk, chunk), chunk)
        slot = t % slots
        return pltpu.make_async_copy(integ.at[t // per_block, :, lanes], panel.at[slot], panel_sem.at[slot])

    raw_copy = pltpu.make_async_copy(amp, raw, raw_sem)

    def gather_copy(h, q, to_col):
        return send(gathered.at[h, q, col], gathered.at[h, q, col], gather_send, gather_recv.at[h, q], row, to_col)

    def peer_copy(t):
        slot = t % peers
        return send(part.at[t, 1 - core], peer.at[slot], peer_send.at[slot], peer_recv.at[slot], mate, col)

    def data_copy(t, way, count, to_row, first):
        slot = t % ring
        return send(stage.at[slot, pl.ds(first, count)], inbox.at[slot, pl.ds(first + 1 - way, count)],
                    stage_send.at[way, slot], inbox_recv.at[way, slot], to_row, col)

    def scale_copy(t, way, to_row):
        slot = t % ring
        return send(scale_out.at[way, slot], scale_in.at[way, slot], scale_send.at[way, slot],
                    scale_recv.at[way, slot], to_row, col)

    def loop(low, high, body):
        lax.fori_loop(low, high, lambda i, c: (body(i), c)[1], 0)

    def when(condition, body, *args):
        @pl.when(condition)
        def _():
            body(*args)

    raw_copy.start()
    for t in range(min(slots, steps)):
        panel_copy(t).start()

    barrier = pltpu.get_barrier_semaphore()

    def greet(to_row, to_col):
        pl.semaphore_signal(barrier, inc=1, device_id={"row": to_row, "col": to_col},
                            device_id_type=pl.DeviceIdType.MESH)

    for shift in shifts:
        greet(row, partner(shift, 1))
    greet(mate, col)
    when(z > 0, greet, row - CORES, col)
    when(z < chips - 1, greet, row + CORES, col)

    def mask(h):
        index = row * span + lax.broadcasted_iota(jnp.int32, (share, span), 1)
        values = jnp.where(index < sizes[h], raw[:, h, :].astype(jnp.float32), 0.0)
        values = values.astype(gathered.dtype)
        for q in range(CORES):
            gathered[h, q, col] = values[q * pairs:(q + 1) * pairs]

    raw_copy.wait()
    mask(0)
    pl.semaphore_wait(barrier, cols + jnp.where(z > 0, 1, 0) + jnp.where(z < chips - 1, 1, 0))

    def scatter(h):
        def one(q):
            for shift in shifts:
                gather_copy(h, q, partner(shift, 1)).start()

        loop(0, CORES, one)

    scatter(0)

    for h in range(1, blocks):
        mask(h)
        scatter(h)

    def collect(h, q):
        others = gathered.at[h, q, pl.ds(0, cols - 1)]
        pltpu.make_async_copy(others, others, gather_recv.at[h, q]).wait()

    def next_panel(t):
        when(t + slots < steps, lambda: panel_copy(t + slots).start())

    def start_peer(t):
        when(t >= peers, lambda: peer_copy(t - peers).wait_send())
        peer_copy(t).start()

    def half(t, q):
        when(t == 0, collect, 0, q)
        when(q == 0, lambda: panel_copy(t).wait())
        left = gathered[0, q].reshape(cols * pairs, span)
        value = jnp.dot(left, panel[t % slots], preferred_element_type=jnp.float32)
        part[t, q] = value.reshape(chips, pairs, chunk)
        when(core != q, start_peer, t)
        when(q == 1, next_panel, t)

    def full(t):
        h = t // per_block
        when(t % per_block == 0, lambda: loop(0, CORES, lambda q: collect(h, q)))
        panel_copy(t).wait()
        left = gathered[h].reshape(CORES * cols * pairs, span)
        value = jnp.dot(left, panel[t % slots], preferred_element_type=jnp.float32)
        part[t] = value.reshape(CORES, chips, pairs, chunk)
        start_peer(t)
        next_panel(t)

    def combine(t):
        peer_copy(t).wait_recv()

        def add(d):
            part[t, core, d] = part[t, core, d] + peer[t % peers, d]

        loop(0, chips, add)

    def fold(value):
        value = jnp.abs(value)
        value = functools.reduce(jnp.maximum, [value[i:i + 8] for i in range(0, pairs, 8)])
        return functools.reduce(jnp.maximum, [value[:, i:i + LANES] for i in range(0, chunk, LANES)])

    def spread(value):
        return jnp.concatenate([value] * (chunk // LANES), axis=1)

    def ahead_of(way):
        return jnp.where(way == 0, chips - 1 - z, z)

    def each_count(count, low, high, body):
        for n in range(low, high):
            when(count == n, body, n)

    def sent_wait(t, way):
        scale_copy(t, way, row).wait_send()
        each_count(ahead_of(way), 1, chips, lambda n: data_copy(t, way, n, row, 0).wait_send())

    def relay(t, way):
        up = way == 0
        has_source = jnp.where(up, z, chips - 1 - z) > 0
        ahead = ahead_of(way)
        to_row = row + CORES - 2 * CORES * way
        first = jnp.where(up, z + 1, 0)
        slot = t % ring

        @pl.when(has_source)
        def _():
            scale_copy(t, way, row).wait_recv()
            each_count(ahead + 1, 1, chips, lambda n: data_copy(t, way, n, row, 0).wait_recv())

        def take(d):
            factor = spread(scale_in[way, slot])
            part[t, core, d] = part[t, core, d] + inbox[slot, d + 1 - way].astype(jnp.int32).astype(jnp.float32) * factor

        when(jnp.logical_and(has_source, ahead > 0), loop, first, first + ahead, take)

        @pl.when(ahead > 0)
        def _():
            when(t >= ring, sent_wait, t - ring, way)
            largest = lax.fori_loop(
                first, first + ahead, lambda d, m: jnp.maximum(m, fold(part[t, core, d])), jnp.full((8, LANES), TINY, jnp.float32))
            largest = jnp.max(largest, axis=0, keepdims=True)
            scale_out[way, slot] = largest * (1.0 / TOP)
            scale_copy(t, way, to_row).start()
            inverse = spread(TOP / largest)

            def put(d):
                stage[slot, d] = jnp.round(part[t, core, d] * inverse).astype(jnp.int32).astype(jnp.int16)

            loop(first, first + ahead, put)
            each_count(ahead, 1, chips, lambda n: data_copy(t, way, n, to_row, first).start())

        when(has_source, take, z)

    def finish(t):
        h = t // per_block
        low = (t % per_block) * chunk
        index = col * width + low + lax.broadcasted_iota(jnp.int32, (pairs, chunk), 1)
        out[:, h, pl.ds(pl.multiple_of(low, chunk), chunk)] = jnp.where(index < sizes[h], part[t, core, z], 0.0)

    def at(j, body):
        ahead = jnp.logical_and(core == 0, j < early)
        t = jnp.where(ahead, j, jnp.where(jnp.logical_and(core == 0, j < 2 * early), -1, j - early))
        when(jnp.logical_and(t >= 0, t < steps), body, t)

    near = jnp.where(2 * z < chips, 0, 1)
    short = jnp.where(2 * z < chips, z, chips - 1 - z)
    near_lag = 1 + LAG * short
    far_lag = 1 + LAG * (chips - 1 - short)
    end_lag = 1 + LAG * (chips - 1)

    def step(i):
        when(jnp.logical_and(i < 2 * early, i != early), lambda: half(i % early, i // early))
        when(jnp.logical_and(i >= 2 * early, i < steps + early), lambda: full(i - early))
        at(i - 1, combine)
        at(i - near_lag, lambda t: relay(t, near))
        at(i - far_lag, lambda t: relay(t, 1 - near))
        at(i - end_lag, finish)
        when(i == early, lambda: half(0, 1))

    loop(0, steps + early + end_lag, step)

    everything = gathered.at[:, :, pl.ds(0, cols - 1)]
    pltpu.make_async_copy(everything, everything, gather_send).wait()
    loop(max(0, steps - peers), steps, lambda t: peer_copy(t).wait_send())

    def drain(t):
        for way in range(2):
            when(ahead_of(way) > 0, sent_wait, t, way)

    loop(max(0, steps - ring), steps, drain)


def body(chips, cols, amplitudes, integrals, block_sizes):
    share, blocks, span = amplitudes.shape
    width = integrals.shape[2]
    chunk = min(CHUNK, width)
    steps = blocks * (width // chunk)
    total = share * cols
    pairs = total // (chips * CORES)
    assert share == CORES * pairs and chips == cols
    slots = min(SLOTS, steps)
    peers = min(2 * SLOTS, steps)
    ring = min(RING, steps)
    dma = pltpu.SemaphoreType.DMA
    result = pl.pallas_call(
        functools.partial(kernel, chips, cols, steps, chunk),
        out_shape=jax.ShapeDtypeStruct((pairs, blocks, width), jnp.float32),
        in_specs=[
            pl.BlockSpec(memory_space=pltpu.SMEM),
            pl.BlockSpec(memory_space=pl.ANY),
            pl.BlockSpec(memory_space=pl.ANY),
        ],
        out_specs=pl.BlockSpec(memory_space=pltpu.VMEM),
        scratch_shapes=[
            pltpu.VMEM((share, blocks, span), amplitudes.dtype),
            pltpu.VMEM((blocks, CORES, cols, pairs, span), amplitudes.dtype),
            pltpu.VMEM((slots, span, chunk), integrals.dtype),
            pltpu.VMEM((steps, CORES, chips, pairs, chunk), jnp.float32),
            pltpu.VMEM((peers, chips, pairs, chunk), jnp.float32),
            pltpu.VMEM((ring, chips, pairs, chunk), jnp.int16),
            pltpu.VMEM((ring, chips + 1, pairs, chunk), jnp.int16),
            pltpu.VMEM((2, ring, 1, LANES), jnp.float32),
            pltpu.VMEM((2, ring, 1, LANES), jnp.float32),
            dma,
            dma,
            dma((blocks, CORES)),
            dma((slots,)),
            dma((peers,)),
            dma((peers,)),
            dma((2, ring)),
            dma((2, ring)),
            dma((2, ring)),
            dma((2, ring)),
        ],
        compiler_params=pltpu.CompilerParams(
            collective_id=0, has_side_effects=True, vmem_limit_bytes=63 * 2**20
        ),
        name="ladder",
    )(block_sizes, amplitudes, integrals)
    return result


def solution(mesh):
    placed = (P("col", None, "row"), P(None, "row", "col"), P())
    return jax.shard_map(
        functools.partial(body, mesh.shape["row"] // CORES, mesh.shape["col"]),
        mesh=mesh, in_specs=placed, out_specs=P("row", None, "col"), check_vma=False,
    )
```

time: 109 us -> 106 us (0.972)
  local copies, waits for them, and re-layouts: 7.03 us -> 3.14 us
  Pallas kernels: 101 us -> 103 us
    transpose x1 -> x0, local copies, waits for them, and re-layouts: 4.26 us -> none  [body(): return result.transpose(1, 0, 2)]
    pallas_call x1, Pallas kernels: 101 us -> 103 us  [body(): pl.pallas_call(functools.partial(kernel, chips, cols, steps, chunk), out_...]
where the time goes in v1:
time: 106 us
  Pallas kernels  103 us (97%)
  local copies, waits for them, and re-layouts  3.14 us (3%)
    pallas_call x1, Pallas kernels, body(): pl.pallas_call(functools.partial(kernel, chips, cols, steps, chunk), out_...  103 us
    unnamed x1, local copies, waits for them, and re-layouts  3.14 us

profile of v1, /device:TPU:0, one launch (start us, length us, event | category | flops | bytes accessed | tf_op | source)
XLA Modules:
  0.0 105.8 jit_solution(3342546309447915664)
XLA Ops:
  0.0 102.7 %ladder.1 = f32[32,4,4096]{2,1,0:T(4,128)} custom-call(s32[4]{0:T(128)} %sizes.1, bf16[64,4,2048]{2,1,0:T(4,128)(2,1)} %amp.1, bf16[4,2048,4096]{2,1,0:T(8,128)(2,1)} %integ.1), custom_call_target="tpu_custom_call" | custom-call | tf_op jit(solution)/shard_map/ladder/pallas_call | solution.py:262
  102.7 3.1 %copy.5 = f32[32,4,4096]{2,1,0:T(4,128)} copy(f32[32,4,4096]{2,1,0:T(4,128)} %ladder.1) | data formatting | bytes 4194304

commit v2 on v1

--- a/solution.py
+++ b/solution.py
@@ -14,19 +14,22 @@
 LANES = 128
 LAG = 3
 RING = 2 * LAG + 6
+DIRECT = 3
 TOP = 32766.0
 TINY = 1e-30
+LIMIT = 63 * 2**20
 
 
 def kernel(chips, cols, steps, chunk, sizes, amp, integ, out, raw, gathered, panel, part, peer, stage, inbox,
-           scale_out, scale_in, raw_sem, gather_send, gather_recv, panel_sem, peer_send, peer_recv,
-           stage_send, inbox_recv, scale_send, scale_recv):
+           scale_out, scale_in, far_stage, far_inbox, far_out, far_in, raw_sem, gather_send, gather_recv, panel_sem, peer_send, peer_recv,
+           stage_send, inbox_recv, scale_send, scale_recv, far_send, far_recv, far_scale_send, far_scale_recv):
     row, col = lax.axis_index("row"), lax.axis_index("col")
     z, core = row // CORES, row % CORES
     share, blocks, span = amp.shape
     pairs = share // CORES
     per_block = steps // blocks
     slots, peers, ring = panel.shape[0], peer.shape[0], stage.shape[0]
+    relayed = steps - far_stage.shape[0]
     early = min(per_block, slots)
     width = chunk * per_block
     mate = z * CORES + 1 - core
@@ -208,16 +211,54 @@
 
         when(has_source, take, z)
 
+    def far_copies(t, d):
+        slot = t - relayed
+        to_row = d * CORES + core
+        return (send(far_out.at[slot, d], far_in.at[slot, z], far_scale_send, far_scale_recv.at[slot], to_row, col),
+                send(far_stage.at[slot, d], far_inbox.at[slot, z], far_send, far_recv.at[slot], to_row, col))
+
+    def spray(t):
+        slot = t - relayed
+
+        def one(j):
+            d = jnp.where(2 * z < chips, chips - 1 - j, j)
+
+            @pl.when(d != z)
+            def _():
+                value = part[t, core, d]
+                largest = jnp.max(jnp.maximum(fold(value), TINY), axis=0, keepdims=True)
+                far_out[slot, d] = largest * (1.0 / TOP)
+                far_stage[slot, d] = jnp.round(value * spread(TOP / largest)).astype(jnp.int32).astype(jnp.int16)
+                for copy in far_copies(t, d):
+                    copy.start()
+
+        loop(0, chips, one)
+
+    def arrived(t):
+        slot = t - relayed
+        for box, sem in ((far_in, far_scale_recv), (far_inbox, far_recv)):
+            others = box.at[slot, pl.ds(0, chips - 1)]
+            pltpu.make_async_copy(others, others, sem.at[slot]).wait()
+
+        def add(source):
+            @pl.when(source != z)
+            def _():
+                value = far_inbox[slot, source].astype(jnp.int32).astype(jnp.float32) * spread(far_in[slot, source])
+                part[t, core, z] = part[t, core, z] + value
+
+        loop(0, chips, add)
+
     def finish(t):
+        when(t >= relayed, arrived, t)
         h = t // per_block
         low = (t % per_block) * chunk
         index = col * width + low + lax.broadcasted_iota(jnp.int32, (pairs, chunk), 1)
         out[:, h, pl.ds(pl.multiple_of(low, chunk), chunk)] = jnp.where(index < sizes[h], part[t, core, z], 0.0)
 
-    def at(j, body):
+    def at(j, low, high, body):
         ahead = jnp.logical_and(core == 0, j < early)
         t = jnp.where(ahead, j, jnp.where(jnp.logical_and(core == 0, j < 2 * early), -1, j - early))
-        when(jnp.logical_and(t >= 0, t < steps), body, t)
+        when(jnp.logical_and(t >= low, t < high), body, t)
 
     near = jnp.where(2 * z < chips, 0, 1)
     short = jnp.where(2 * z < chips, z, chips - 1 - z)
@@ -228,10 +269,11 @@
     def step(i):
         when(jnp.logical_and(i < 2 * early, i != early), lambda: half(i % early, i // early))
         when(jnp.logical_and(i >= 2 * early, i < steps + early), lambda: full(i - early))
-        at(i - 1, combine)
-        at(i - near_lag, lambda t: relay(t, near))
-        at(i - far_lag, lambda t: relay(t, 1 - near))
-        at(i - end_lag, finish)
+        at(i - 1, 0, steps, combine)
+        at(i - 1, relayed, steps, spray)
+        at(i - near_lag, 0, relayed, lambda t: relay(t, near))
+        at(i - far_lag, 0, relayed, lambda t: relay(t, 1 - near))
+        at(i - end_lag, 0, steps, finish)
         when(i == early, lambda: half(0, 1))
 
     loop(0, steps + early + end_lag, step)
@@ -244,7 +286,10 @@
         for way in range(2):
             when(ahead_of(way) > 0, sent_wait, t, way)
 
-    loop(max(0, steps - ring), steps, drain)
+    loop(max(0, relayed - ring), relayed, drain)
+    for box, sem in ((far_in, far_scale_send), (far_inbox, far_send)):
+        others = box.at[:, pl.ds(0, chips - 1)]
+        pltpu.make_async_copy(others, others, sem).wait()
 
 
 def body(chips, cols, amplitudes, integrals, block_sizes):
@@ -258,6 +303,7 @@
     slots = min(SLOTS, steps)
     peers = min(2 * SLOTS, steps)
     ring = min(RING, steps)
+    direct = min(DIRECT, steps)
     dma = pltpu.SemaphoreType.DMA
     result = pl.pallas_call(
         functools.partial(kernel, chips, cols, steps, chunk),
@@ -278,6 +324,10 @@
             pltpu.VMEM((ring, chips + 1, pairs, chunk), jnp.int16),
             pltpu.VMEM((2, ring, 1, LANES), jnp.float32),
             pltpu.VMEM((2, ring, 1, LANES), jnp.float32),
+            pltpu.VMEM((direct, chips, pairs, chunk), jnp.int16),
+            pltpu.VMEM((direct, chips, pairs, chunk), jnp.int16),
+            pltpu.VMEM((direct, chips, 1, LANES), jnp.float32),
+            pltpu.VMEM((direct, chips, 1, LANES), jnp.float32),
             dma,
             dma,
             dma((blocks, CORES)),
@@ -288,9 +338,13 @@
             dma((2, ring)),
             dma((2, ring)),
             dma((2, ring)),
+            dma,
+            dma((direct,)),
+            dma,
+            dma((direct,)),
         ],
         compiler_params=pltpu.CompilerParams(
-            collective_id=0, has_side_effects=True, vmem_limit_bytes=63 * 2**20
+            collective_id=0, has_side_effects=True, vmem_limit_bytes=LIMIT
         ),
         name="ladder",
     )(block_sizes, amplitudes, integrals)

time: 106 us -> 107 us (level)
  no operation moved by 1% of the time
where the time goes in v2:
time: 107 us
  Pallas kernels  103 us (96%)
  local copies, waits for them, and re-layouts  3.14 us (3%)
    pallas_call x1, Pallas kernels, body(): pl.pallas_call(functools.partial(kernel, chips, cols, steps, chunk), out_...  103 us
    unnamed x1, local copies, waits for them, and re-layouts  3.14 us

profile of v2, /device:TPU:0, one launch (start us, length us, event | category | flops | bytes accessed | tf_op | source)
XLA Modules:
  0.0 106.5 jit_solution(8628516480354782180)
XLA Ops:
  0.0 103.4 %ladder.1 = f32[32,4,4096]{2,1,0:T(4,128)} custom-call(s32[4]{0:T(128)} %sizes.1, bf16[64,4,2048]{2,1,0:T(4,128)(2,1)} %amp.1, bf16[4,2048,4096]{2,1,0:T(8,128)(2,1)} %integ.1), custom_call_target="tpu_custom_call" | custom-call | tf_op jit(solution)/shard_map/ladder/pallas_call | solution.py:308
  103.4 3.1 %copy.5 = f32[32,4,4096]{2,1,0:T(4,128)} copy(f32[32,4,4096]{2,1,0:T(4,128)} %ladder.1) | data formatting | bytes 4194304
